TPU v7x, 256 devices: a whole 4x4x8 slice. The times are simulated.
256 devices in a mesh: row: 16 (over z, x_lo), col: 8 (over x_hi, y), depth: 2 (over core).
Axes of the slice: x: 4 (x_hi: 2, x_lo: 2; x = x_hi * 2 + x_lo), y: 4, z: 8, core: 2. Of those that a mesh axis runs over, the one named last changes fastest.
Arguments:
- row_slab: bfloat16 [2048, 53248], P('row', ('col', 'depth')), may hold values from -6 to 6
- col_slab: bfloat16 [53248, 4096], P('row', ('col', 'depth')), may hold values from -0.046875 to 0.046875
- row_occupied: int32 [16, 416], P('row', ('col', 'depth')), may hold values 0 or 1
- col_occupied: int32 [416, 32], P('row', ('col', 'depth')), may hold values 0 or 1
- keep_mask: int32 [16, 32], P('row', ('col', 'depth')), may hold values 0 or 1
Outputs:
- squared: bfloat16 [2048, 4096], P('row', ('col', 'depth'))
All inputs are finite; a program needn't handle non-finite values. No bound on the sum of `row_occupied` or of `col_occupied` or of `keep_mask` on one device may be relied on, other than what follows from the above.
Results may differ from a plain program's by a relative error of at most 0.001.
Values may be sent and summed in bfloat16 or wider, within the bound.
No kernel may reach another device: no remote copies, remote signals or barrier semaphores. Data moves between devices by JAX's collectives and lax.ppermute only.
A program may use at most 192 MiB of HBM per device.

v0:
```python
import jax
import jax.numpy as jnp
from jax import lax
from jax.sharding import PartitionSpec as P

BLK = 128


def masked(matrix, occupied):
    row_count = matrix.shape[0] // BLK
    col_count = matrix.shape[1] // BLK
    blocks = (
        matrix.reshape(row_count, BLK, col_count, BLK)
        * occupied.astype(matrix.dtype)[:, None, :, None]
    )
    return blocks.reshape(matrix.shape)


def local(row_slab, col_slab, row_occupied, col_occupied, keep_mask):
    whole_rows, whole_row_occ = (
        lax.all_gather(row_slab, ("col", "depth"), axis=1, tiled=True),
        lax.all_gather(row_occupied, ("col", "depth"), axis=1, tiled=True),
    )
    left_band = masked(whole_rows, whole_row_occ)
    segment = masked(
        lax.all_gather(col_slab, "row", axis=0, tiled=True),
        lax.all_gather(col_occupied, "row", axis=0, tiled=True),
    )
    product = jnp.dot(left_band, segment, preferred_element_type=jnp.float32)
    return masked(product, keep_mask).astype(jnp.bfloat16)


def solution(mesh):
    placed = (
        P("row", ("col", "depth")),
        P("row", ("col", "depth")),
        P("row", ("col", "depth")),
        P("row", ("col", "depth")),
        P("row", ("col", "depth")),
    )
    return jax.shard_map(
        local, mesh=mesh, in_specs=placed, out_specs=P("row", ("col", "depth")), check_vma=False
    )
```

profile of v0, /device:TPU:1, one launch (start us, length us, event | category | flops | bytes accessed | tf_op | source)
XLA Modules:
  0.0 702.5 jit_solution(5745444827072541923)
XLA Ops:
  6.5 0.0 all-gather.6.cloned.1.call-start
  6.5 0.7 all-gather.6.cloned.1.call-update
  7.3 0.0 all-gather.4.cloned.1.call-start
  7.3 0.7 all-gather.4.cloned.1.call-update
  8.0 45.2 %all-gather = s32[16,26,2]{1,2,0:T(2,128)S(1)} all-gather(s32[1,26,2]{1,2,0:T(2,128)} %bitcast.31), channel_id=1, replica_groups=mesh['row'=16,'col'=8,'depth'=2] {'row'}, dimensions={0}, use_global_device_ids=true | all-gather | bytes 3536 | tf_op jit(solution)/shard_map/all_gather | solution.py:27
  53.2 0.1 reshape.29
  53.3 0.2 copy.13
  53.5 1.3 dynamic-slice
  55.4 0.8 bitcast_dynamic-update-slice_fusion
  56.2 22.9 %all-reduce = s32[416]{0:T(512)S(1)} all-reduce(s32[416]{0:T(512)S(1)} %bitcast_dynamic-update-slice_fusion), channel_id=1, replica_groups=mesh['row'=16,'col'=8,'depth'=2] {'col','depth'}, use_global_device_ids=true, to_apply=%add | all-reduce | flops 416 | bytes 3328
  79.1 0.7 convert_bitcast_fusion
  79.8 0.1 broadcast_bitcast_fusion
  79.9 494.8 %all-gather.6.cloned.1.call-done = bf16[53248,256]{1,0:T(8,128)(2,1)} async-done(((bf16[3328,256]{1,0:T(8,128)(2,1)}), bf16[53248,256]{1,0:T(8,128)(2,1)}) %all-gather.6.cloned.1.call-update) | async-done | bytes 27262992 | tf_op jit(solution)/shard_map/all_gather | solution.py:26
  574.7 19.1 %mul.44 = bf16[416,128,2,128]{3,2,1,0:T(2,128)(2,1)} broadcast(bf16[416,2]{1,0:T(8,128)(2,1)S(1)} %copy.13), dimensions={0,2} | broadcast | bytes 27264640 | tf_op jit(solution)/shard_map/mul | solution.py:13
  593.8 27.7 %fusion = bf16[256,53248]{0,1:T(8,128)(2,1)} fusion(bf16[53248,256]{1,0:T(8,128)(2,1)} %all-gather.6.cloned.1.call-done, bf16[6656,8,2,128]{3,2,1,0:T(2,128)(2,1)} %bitcast.28), kind=kLoop, calls=%fused_computation.1 | loop fusion | flops 13631488 | bytes 81788928 | tf_op jit(solution)/shard_map/dot_general | solution.py:29
  621.5 32.5 %copy.16 = bf16[256,53248]{1,0:T(8,128)(2,1)} copy(bf16[256,53248]{0,1:T(8,128)(2,1)} %fusion) | data formatting | bytes 54525952 | tf_op jit(solution)/shard_map/dot_general | solution.py:29
  654.0 24.6 %all-gather.4.cloned.1.call-done = bf16[128,53248]{1,0:T(8,128)(2,1)} async-done(((bf16[128,3328]{1,0:T(8,128)(2,1)}), bf16[128,53248]{1,0:T(8,128)(2,1)}) %all-gather.4.cloned.1.call-update) | async-done | bytes 13631504 | tf_op jit(solution)/shard_map/all_gather | solution.py:21
  678.6 16.4 %fusion.8 = bf16[128,2,128]{0,2,1:T(8,128)(2,1)S(1)} fusion(bf16[2,128,53248]{2,1,0:T(8,128)(2,1)} %bitcast.29, bf16[128,53248]{1,0:T(8,128)(2,1)} %all-gather.4.cloned.1.call-done, bf16[53248]{0:T(1024)(128)(2,1)S(1)} %broadcast_bitcast_fusion, f32[2]{0:T(128)S(1)} %convert_bitcast_fusion), kind=kOutput, calls=%fused_computation.7 | convolution fusion | flops 3516989440 | bytes 41066504 | tf_op jit(solution)/shard_map/dot_general | solution.py:29
  695.0 0.7 copy.15
  (4 shorter events, 0.0 us)
Async XLA Ops:
  6.5 568.1 %all-gather.6.cloned.1.call-start = ((), (), s32[]{:S(2)}) async-start(), calls=%async_computation.1 | async-start | bytes 28966912 | tf_op jit(solution)/shard_map/all_gather | solution.py:26
  7.3 671.3 %all-gather.4.cloned.1.call-start = ((), (), s32[]{:S(2)}) async-start(), calls=%async_computation | async-start | bytes 14483456 | tf_op jit(solution)/shard_map/all_gather | solution.py:21
Sparse Core Ops, SparseCore 0:
  9.1 565.4 all-gather.5
  577.4 101.1 all-gather.3
where the time goes:
time: 704 us; the launch traced here: 703 us
  waiting for transfers between devices  521 us (74%)
  blocking collectives  68.1 us (10%)
  local copies, waits for them, and re-layouts  54.8 us (8%)
  other arithmetic  28.4 us (4%)
  matrix products  16.4 us (2%)
  between operations  14.1 us (2%)
    all_gather x1, waiting for transfers between devices, local(): lax.all_gather(col_slab, 'row', axis=0, tiled=True)  495 us
    all_gather x1, blocking collectives, local(): lax.all_gather(col_occupied, 'row', axis=0, tiled=True)  45.2 us
    dot_general x1, local copies, waits for them, and re-layouts, local(): product = jnp.dot(left_band, segment, preferred_element_type=jnp.float32)  32.5 us
    dot_general x1, other arithmetic, local(): product = jnp.dot(left_band, segment, preferred_element_type=jnp.float32)  27.7 us
    all_gather x1, waiting for transfers between devices, local(): lax.all_gather(row_slab, ('col', 'depth'), axis=1, tiled=True)  24.6 us
    unnamed x1, blocking collectives  22.9 us
    mul x2, local copies, waits for them, and re-layouts, masked(): matrix.reshape(row_count, BLK, col_count, BLK)  19.3 us
    dot_general x1, matrix products, local(): product = jnp.dot(left_band, segment, preferred_element_type=jnp.float32)  16.4 us
  transfers between devices with their start and end apart: 2, of which 2 were waited for; matrix products, arithmetic and copies ran while one was open for 12% of the time, Pallas kernels for 0%

commit v1 on v0

--- a/solution.py
+++ b/solution.py
@@ -23,7 +23,9 @@
     )
     left_band = masked(whole_rows, whole_row_occ)
     segment = masked(
-        lax.all_gather(col_slab, "row", axis=0, tiled=True),
+        jnp.concatenate(
+            lax.all_to_all(jnp.stack([col_slab] * lax.axis_size("row")), "row", 0, 0), axis=0
+        ),
         lax.all_gather(col_occupied, "row", axis=0, tiled=True),
     )
     product = jnp.dot(left_band, segment, preferred_element_type=jnp.float32)

time: 704 us -> 825 us (1.17)
  blocking collectives: 68.1 us -> 654 us
  waiting for transfers between devices: 521 us -> 0.69 us
  local copies, waits for them, and re-layouts: 54.8 us -> 99.5 us
  starting transfers between devices: 0.04 us -> 10.3 us
    all_gather x1, blocking collectives: 45.2 us -> 637 us  [local(): lax.all_gather(col_occupied, 'row', axis=0, tiled=True)]
    all_gather x1 -> x0, waiting for transfers between devices: 495 us -> none  [local(): lax.all_gather(col_slab, 'row', axis=0, tiled=True)]
    all_to_all x0 -> x1, local copies, waits for them, and re-layouts: none -> 33.3 us  [local(): lax.all_to_all(jnp.stack([col_slab] * lax.axis_size('row')), 'row', 0, 0)]
    all_gather x1, waiting for transfers between devices: 24.6 us -> 0.01 us  [local(): lax.all_gather(row_slab, ('col', 'depth'), axis=1, tiled=True)]
    all_to_all x0 -> x1, starting transfers between devices: none -> 10.2 us  [local(): lax.all_to_all(jnp.stack([col_slab] * lax.axis_size('row')), 'row', 0, 0)]
    another operation x0 -> x1, local copies, waits for them, and re-layouts: none -> 9.39 us  [local(): jnp.stack([col_slab] * lax.axis_size('row'))]
  transfers between devices with their start and end apart: 2 -> 2, of which waited for: 2 -> 0; matrix products, arithmetic and copies ran while one was open for 12% -> 14% of each run, Pallas kernels for 0% -> 0%
where the time goes in v1:
time: 825 us; the launch traced here: 823 us
  blocking collectives  654 us (79%)
  local copies, waits for them, and re-layouts  99.5 us (12%)
  other arithmetic  27.7 us (3%)
  matrix products  16.5 us (2%)
  between operations  14.2 us (2%)
  starting transfers between devices  10.3 us (1%)
    all_gather x1, blocking collectives, local(): lax.all_gather(col_occupied, 'row', axis=0, tiled=True)  637 us
    all_to_all x1, local copies, waits for them, and re-layouts, local(): lax.all_to_all(jnp.stack([col_slab] * lax.axis_size('row')), 'row', 0, 0)  33.3 us
    dot_general x1, local copies, waits for them, and re-layouts, local(): product = jnp.dot(left_band, segment, preferred_element_type=jnp.float32)  33 us
    dot_general x1, other arithmetic, local(): product = jnp.dot(left_band, segment, preferred_element_type=jnp.float32)  27.6 us
    mul x2, local copies, waits for them, and re-layouts, masked(): matrix.reshape(row_count, BLK, col_count, BLK)  19.3 us
    unnamed x1, blocking collectives  17.3 us
    dot_general x1, matrix products, local(): product = jnp.dot(left_band, segment, preferred_element_type=jnp.float32)  16.5 us
  transfers between devices with their start and end apart: 2, of which 0 were waited for; matrix products, arithmetic and copies ran while one was open for 14% of the time, Pallas kernels for 0%

profile of v1, /device:TPU:1, one launch (start us, length us, event | category | flops | bytes accessed | tf_op | source)
XLA Modules:
  0.0 822.8 jit_solution(12006194050198091246)
XLA Ops:
  6.5 2.7 copy.14
  9.3 9.4 %stack.2 = bf16[16,3328,256]{1,2,0:T(8,128)(2,1)} broadcast(bf16[3328,256]{0,1:T(8,128)(2,1)S(1)} %copy.14), dimensions={1,2} | broadcast | bytes 28966912 | tf_op jit(solution)/shard_map/stack | solution.py:27
  18.7 0.0 copy-start
  18.7 0.0 copy-start.3
  18.7 0.0 copy-start.1
  18.7 0.0 copy-start.2
  18.7 10.2 %all-to-all-start = ((bf16[16,3328,256]{1,2,0:T(8,128)(2,1)}), bf16[16,3328,256]{1,2,0:T(8,128)(2,1)}, u32[]{:S(2)}, u32[]{:S(2)}) async-start(bf16[16,3328,256]{1,2,0:T(8,128)(2,1)} %stack.2), calls=%async_computation | async-start | bytes 54525952 | tf_op jit(solution)/shard_map/all_to_all | solution.py:27
  28.9 0.0 all-gather.3.cloned.1.call-start
  29.0 0.7 all-gather.3.cloned.1.call-update
  29.7 0.0 copy-done
  29.7 636.7 %all-gather = s32[16,26,2]{1,2,0:T(2,128)S(1)} all-gather(s32[1,26,2]{1,2,0:T(2,128)S(1)} %bitcast.33), channel_id=1, replica_groups=mesh['row'=16,'col'=8,'depth'=2] {'row'}, dimensions={0}, use_global_device_ids=true | all-gather | bytes 3536 | tf_op jit(solution)/shard_map/all_gather | solution.py:29
  666.4 0.1 reshape.31
  666.5 0.2 copy.17
  666.7 0.0 copy-done.3
  666.7 0.6 dynamic-slice
  668.0 0.0 copy-done.1
  668.0 0.1 bitcast_dynamic-update-slice_fusion
  668.1 17.3 %all-reduce = s32[416]{0:T(512)S(1)} all-reduce(s32[416]{0:T(512)S(1)} %bitcast_dynamic-update-slice_fusion), channel_id=1, replica_groups=mesh['row'=16,'col'=8,'depth'=2] {'col','depth'}, use_global_device_ids=true, to_apply=%add | all-reduce | flops 416 | bytes 3328
  685.4 0.0 copy-done.2
  685.4 0.1 broadcast_bitcast_fusion
  685.5 0.0 all-to-all-done
  685.5 33.3 %copy.15 = bf16[16,3328,256]{2,1,0:T(8,128)(2,1)} copy(bf16[16,3328,256]{1,2,0:T(8,128)(2,1)} %all-to-all-done) | data formatting | bytes 54525952 | tf_op jit(solution)/shard_map/all_to_all | solution.py:27
  718.9 19.1 %mul.44 = bf16[416,128,2,128]{3,2,1,0:T(2,128)(2,1)} broadcast(bf16[416,2]{1,0:T(8,128)(2,1)S(1)} %copy.17), dimensions={0,2} | broadcast | bytes 27264640 | tf_op jit(solution)/shard_map/mul | solution.py:13
  738.0 27.6 %fusion = bf16[256,53248]{0,1:T(8,128)(2,1)} fusion(bf16[6656,8,2,128]{3,2,1,0:T(2,128)(2,1)} %bitcast.30, bf16[16,3328,256]{2,1,0:T(8,128)(2,1)} %copy.15), kind=kLoop, calls=%fused_computation.1 | loop fusion | flops 13631488 | bytes 81788928 | tf_op jit(solution)/shard_map/dot_general | solution.py:31
  765.6 33.0 %copy.20 = bf16[256,53248]{1,0:T(8,128)(2,1)} copy(bf16[256,53248]{0,1:T(8,128)(2,1)} %fusion) | data formatting | bytes 54525952 | tf_op jit(solution)/shard_map/dot_general | solution.py:31
  798.7 0.0 all-gather.3.cloned.1.call-done
  798.7 16.5 %fusion.8 = bf16[128,2,128]{0,2,1:T(8,128)(2,1)S(1)} fusion(bf16[2,128,53248]{2,1,0:T(8,128)(2,1)} %bitcast.31, bf16[128,53248]{1,0:T(8,128)(2,1)} %all-gather.3.cloned.1.call-done, bf16[53248]{0:T(1024)(128)(2,1)S(1)} %broadcast_bitcast_fusion, f32[2]{0:T(128)S(1)} %convert_bitcast_fusion), kind=kOutput, calls=%fused_computation.7 | convolution fusion | flops 3516989440 | bytes 41066504 | tf_op jit(solution)/shard_map/dot_general | solution.py:31
  815.2 0.7 copy.19
  (5 shorter events, 0.0 us)
Async XLA Ops:
  18.7 11.0 %copy-start = (s32[26,2]{0,1:T(2,128)S(1)}, s32[26,2]{0,1:T(2,128)}, u32[]{:S(2)}) copy-start(s32[26,2]{0,1:T(2,128)} %param.8) | copy-start | bytes 628
  18.7 648.0 %copy-start.3 = (u32[256]{0:T(256)S(1)}, u32[256]{0:T(256)}, u32[]{:S(2)}) copy-start(u32[256]{0:T(256)} %constant.5) | copy-start | bytes 3076
  18.7 649.3 %copy-start.1 = (s32[1,26]{1,0:T(1,128)S(1)}, s32[1,26]{1,0:T(1,128)}, u32[]{:S(2)}) copy-start(s32[1,26]{1,0:T(1,128)} %param.7) | copy-start | bytes 316
  18.7 666.7 %copy-start.2 = (s32[1,2]{1,0:T(1,128)S(1)}, s32[1,2]{1,0:T(1,128)}, u32[]{:S(2)}) copy-start(s32[1,2]{1,0:T(1,128)} %param.9) | copy-start | bytes 28
  18.7 666.9 %all-to-all-start = ((bf16[16,3328,256]{1,2,0:T(8,128)(2,1)}), bf16[16,3328,256]{1,2,0:T(8,128)(2,1)}, u32[]{:S(2)}, u32[]{:S(2)}) async-start(bf16[16,3328,256]{1,2,0:T(8,128)(2,1)} %stack.2), calls=%async_computation | async-start | bytes 54525952 | tf_op jit(solution)/shard_map/all_to_all | solution.py:27
  28.9 769.8 %all-gather.3.cloned.1.call-start = ((), (), s32[]{:S(2)}) async-start(), calls=%async_computation.1 | async-start | bytes 14483456 | tf_op jit(solution)/shard_map/all_gather | solution.py:21
Sparse Core Ops, SparseCore 0:
  32.5 110.8 all-gather.2
